TPU v7x, 32 devices: a whole 2x2x4 slice. The times are simulated.
32 devices in a mesh: parts: 2 (over x), tm: 16 (over z, y, core).
Axes of the slice: x: 2, y: 2, z: 4, core: 2. Of those that a mesh axis runs over, the one named last changes fastest.
Arguments:
- query_states: bfloat16 [32, 384, 768], P(('parts', 'tm')), parts along dimension 0, may hold values from -88 to 88
- key_states: bfloat16 [32, 384, 768], P(('parts', 'tm')), parts along dimension 0, may hold values from -4 to 4
- value_states: bfloat16 [32, 384, 768], P(('parts', 'tm')), parts along dimension 0, may hold values from -40 to 40
- out_weight: bfloat16 [1536, 3072], replicated, may hold values from -0.15625 to 0.15625
Outputs:
- mixed: bfloat16 [6144, 3072], P(('parts', 'tm')), parts along dimension 0
There are 2 independent parts, one for each index of `parts`. A program takes and returns all parts, laid end to end along the dimension named above; an argument that names none is the same for every part. Nothing has to cross between parts.
All inputs are finite; a program needn't handle non-finite values.
Results may differ from a plain program's by a relative error of at most 0.0058.
Values may be sent and summed in bfloat16 or wider, within the bound.
A program may use at most 128 MiB of HBM per device.

v0:
```python
import functools

import jax
import jax.numpy as jnp
from jax import lax
from jax.experimental import pallas as pl
from jax.experimental.pallas import tpu as pltpu
from jax.sharding import PartitionSpec as P

TCOLS = 4
HD = 128
MESH = pl.DeviceIdType.MESH
LOG2E = 1.4426950408889634

DIRECT_OWN = 2
DIRECT_CORNER = 1
AHEAD = 2
LAG_TIME = 2
LAG_CORNER = 3
LAG_MIDDLE = 5


def slot_of(time_step, col_step):
    return (time_step + 1) * 3 + col_step + 1


def kernel(
    time_count,
    heads,
    q_hbm,
    k_hbm,
    v_hbm,
    w_hbm,
    out_ref,
    q_s,
    kv,
    w_s,
    m_s,
    l_s,
    acc_s,
    outgoing,
    attended,
    load_sem,
    w_sem,
    send_sem,
    recv_sem,
    att_send_sem,
    att_recv_sem,
):
    rows = q_s.shape[1]
    half = rows // 2
    me = lax.axis_index("tm")
    group = lax.rem(me, 2)
    tile = lax.div(me, 2)
    col = lax.rem(tile, TCOLS)
    time = lax.div(tile, TCOLS)
    has_time = {-1: time > 0, 1: time < time_count - 1}
    has_col = {-1: col > 0, 1: col < TCOLS - 1}
    outer = 1 - 2 * lax.rem(col, 2)
    is_edge = jnp.logical_or(col == 0, col == TCOLS - 1)
    is_middle = jnp.logical_not(is_edge)
    outer_device = me + 2 * outer
    middle_device = me - 2 * outer
    relay_device = me + 4 * outer
    other_core = me + 1 - 2 * group
    own_slot = slot_of(0, 0)
    stride = TCOLS
    has_hop = {-1: tile >= stride // 2, 1: tile + stride // 2 < time_count * TCOLS}
    is_hop = jnp.logical_and(has_hop[-1], has_hop[1])

    def hop_slot(step):
        return 9 if step < 0 else 10

    def load(h):
        columns = pl.ds(pl.multiple_of(h * HD, HD), HD)
        return (
            pltpu.make_async_copy(k_hbm.at[0, :, columns], kv.at[own_slot, h, 0], load_sem.at[0, h]),
            pltpu.make_async_copy(v_hbm.at[0, :, columns], kv.at[own_slot, h, 1], load_sem.at[1, h]),
            pltpu.make_async_copy(q_hbm.at[0, :, columns], q_s.at[h], load_sem.at[2, h]),
        )

    for h in range(heads):
        for copy in load(jnp.int32(h)):
            copy.start()
    w_copy = pltpu.make_async_copy(w_hbm, w_s, w_sem)
    w_copy.start()

    barrier = pltpu.get_barrier_semaphore()

    def greet(device):
        pl.semaphore_signal(barrier, inc=1, device_id={"tm": device}, device_id_type=MESH)

    greetings = jnp.int32(2)
    greet(other_core)
    greet(outer_device)
    for step in (-1, 1):
        pl.when(has_hop[step])(lambda step=step: greet(me + stride * step))
        greetings = greetings + has_hop[step].astype(jnp.int32)
    pl.when(is_middle)(lambda: greet(middle_device))
    greetings = greetings + is_middle.astype(jnp.int32)
    pl.semaphore_wait(barrier, greetings)

    def transfer(kind, h, source, target, device):
        return pltpu.make_async_remote_copy(
            src_ref=kv.at[source, h],
            dst_ref=kv.at[target, h],
            send_sem=send_sem.at[kind, h],
            recv_sem=recv_sem.at[target, h],
            device_id={"tm": device},
            device_id_type=MESH,
        )

    def arrive(slot, h):
        transfer(0, h, slot, slot, other_core).wait_recv()

    def send_time(step, h):
        return transfer(0 if step < 0 else 1, h, own_slot, hop_slot(step), me + stride * step)

    def send_hop(step, h):
        return transfer(11 if step < 0 else 12, h, hop_slot(step), slot_of(-step, 0), me + stride * step)

    def send_outer(step, h):
        return transfer(3 + step, h, slot_of(step, 0), slot_of(step, 0) - outer, outer_device)

    def send_middle(step, h):
        return transfer(6 + step, h, slot_of(step, 0), slot_of(step, 0) + outer, middle_device)

    def send_relay(step, h):
        return transfer(9 + step, h, slot_of(step, 0) + outer, slot_of(step, 0) - outer, relay_device)

    def straight(step, h):
        return h >= heads - (DIRECT_OWN if step == 0 else DIRECT_CORNER)

    def send_att(h):
        return pltpu.make_async_remote_copy(
            src_ref=outgoing.at[h],
            dst_ref=attended.at[group, h],
            send_sem=att_send_sem.at[h],
            recv_sem=att_recv_sem.at[h],
            device_id={"tm": other_core},
            device_id_type=MESH,
        )

    def recv_att(h):
        return pltpu.make_async_remote_copy(
            src_ref=outgoing.at[h],
            dst_ref=attended.at[1 - group, h],
            send_sem=att_send_sem.at[h],
            recv_sem=att_recv_sem.at[h],
            device_id={"tm": other_core},
            device_id_type=MESH,
        )

    def send_own(h):
        for copy in load(h):
            copy.wait()
        for step in (-1, 1):
            pl.when(has_time[step])(lambda step=step: send_time(step, h).start())
        send_outer(0, h).start()
        if DIRECT_OWN:
            pl.when(jnp.logical_and(is_middle, straight(0, h)))(lambda: send_middle(0, h).start())

    for h in range(AHEAD):
        send_own(jnp.int32(h))

    exponent_scale = (HD ** (-0.5)) * LOG2E

    def attend(slot, h, first=False):
        scores = lax.dot_general(
            q_s[h], kv[slot, h, 0], (((1,), (1,)), ((), ())), preferred_element_type=jnp.float32
        )
        row_max = jnp.max(scores, axis=1, keepdims=True)
        if not first:
            old_max = m_s[h][:, :1]
            row_max = jnp.maximum(row_max, old_max)
        weights = jnp.exp2((scores - row_max) * exponent_scale)
        total = jnp.sum(weights, axis=1, keepdims=True)
        result = jnp.dot(weights.astype(jnp.bfloat16), kv[slot, h, 1], preferred_element_type=jnp.float32)
        if not first:
            keep = jnp.exp2((old_max - row_max) * exponent_scale)
            total = total + keep * l_s[h][:, :1]
            result = result + keep * acc_s[h]
        m_s[h] = jnp.broadcast_to(row_max, (rows, HD))
        l_s[h] = jnp.broadcast_to(total, (rows, HD))
        acc_s[h] = result

    def finish(h):
        acc_s[h] = acc_s[h] / l_s[h]
        attended[group, h] = acc_s[h, pl.ds(pl.multiple_of(group * half, 16), half), :].astype(jnp.bfloat16)
        outgoing[h] = acc_s[h, pl.ds(pl.multiple_of((1 - group) * half, 16), half), :].astype(jnp.bfloat16)

    def ready(h):
        return jnp.logical_and(h >= 0, h < heads)

    @pl.loop(0, heads + LAG_MIDDLE)
    def _(i):
        pl.when(i + AHEAD < heads)(lambda: send_own(i + AHEAD))

        @pl.when(jnp.logical_and(i < heads, is_edge))
        def _():
            arrive(own_slot + outer, i)
            pl.when(jnp.logical_not(straight(0, i)))(lambda: send_relay(0, i).start())

        @pl.when(jnp.logical_and(i < heads, is_hop))
        def _():
            for step in (-1, 1):
                arrive(hop_slot(step), i)
                send_hop(step, i).start()

        crossed = i - LAG_TIME

        @pl.when(ready(crossed))
        def _():
            for step in (-1, 1):

                @pl.when(has_time[step])
                def _():
                    arrive(slot_of(step, 0), crossed)
                    send_outer(step, crossed).start()
                    if DIRECT_CORNER:
                        pl.when(jnp.logical_and(is_middle, straight(step, crossed)))(
                            lambda: send_middle(step, crossed).start()
                        )

        back = i - LAG_CORNER

        @pl.when(jnp.logical_and(ready(back), is_edge))
        def _():
            for step in (-1, 1):

                @pl.when(has_time[step])
                def _():
                    arrive(slot_of(step, 0) + outer, back)
                    pl.when(jnp.logical_not(straight(step, back)))(lambda: send_relay(step, back).start())

        pl.when(i < heads)(lambda: attend(own_slot, i, first=True))

        @pl.when(ready(crossed))
        def _():
            for step in (-1, 1):
                pl.when(has_time[step])(lambda: attend(slot_of(step, 0), crossed))

        @pl.when(ready(back))
        def _():
            pl.when(is_middle)(lambda: arrive(own_slot + outer, back))
            attend(own_slot + outer, back)
            for step in (-1, 1):

                @pl.when(has_time[step])
                def _():
                    pl.when(is_middle)(lambda: arrive(slot_of(step, 0) + outer, back))
                    attend(slot_of(step, 0) + outer, back)

        last = i - LAG_MIDDLE

        @pl.when(last >= 1)
        def _():
            send_att(last - 1).start()

        @pl.when(last >= 0)
        def _():
            @pl.when(is_middle)
            def _():
                arrive(own_slot - outer, last)
                attend(own_slot - outer, last)
                for step in (-1, 1):

                    @pl.when(has_time[step])
                    def _():
                        arrive(slot_of(step, 0) - outer, last)
                        attend(slot_of(step, 0) - outer, last)

            finish(last)

    send_att(heads - 1).start()
    w_copy.wait()

    for h in range(heads):
        recv_att(h).wait_recv()

    width = out_ref.shape[1]
    chunk = 512
    lhs = jnp.concatenate([attended[part, h] for part in range(2) for h in range(heads)], axis=1)

    @pl.loop(0, width // chunk, unroll=True)
    def _(n):
        columns = pl.ds(pl.multiple_of(n * chunk, chunk), chunk)
        out_ref[:, columns] = jnp.dot(lhs, w_s[:, columns], preferred_element_type=jnp.float32).astype(
            out_ref.dtype
        )

    @pl.loop(0, heads)
    def _(h):
        send_att(h).wait_send()
        send_outer(0, h).wait_send()

        @pl.when(is_hop)
        def _():
            for step in (-1, 1):
                send_hop(step, h).wait_send()

        if DIRECT_OWN:
            pl.when(jnp.logical_and(is_middle, straight(0, h)))(lambda: send_middle(0, h).wait_send())
        pl.when(jnp.logical_and(is_edge, jnp.logical_not(straight(0, h))))(
            lambda: send_relay(0, h).wait_send()
        )
        for step in (-1, 1):

            @pl.when(has_time[step])
            def _():
                send_time(step, h).wait_send()
                send_outer(step, h).wait_send()
                if DIRECT_CORNER:
                    pl.when(jnp.logical_and(is_middle, straight(step, h)))(
                        lambda: send_middle(step, h).wait_send()
                    )
                pl.when(jnp.logical_and(is_edge, jnp.logical_not(straight(step, h))))(
                    lambda: send_relay(step, h).wait_send()
                )


def per_device(query_states, key_states, value_states, out_weight):
    rows, half_width = query_states.shape[1:]
    heads = half_width // HD
    depth, width = out_weight.shape
    time_count = lax.axis_size("tm") // (2 * TCOLS)
    return pl.pallas_call(
        functools.partial(kernel, time_count, heads),
        out_shape=jax.ShapeDtypeStruct((rows // 2, width), jnp.bfloat16),
        in_specs=[pl.BlockSpec(memory_space=pl.ANY)] * 4,
        out_specs=pl.BlockSpec(memory_space=pltpu.VMEM),
        scratch_shapes=[
            pltpu.VMEM((heads, rows, HD), jnp.bfloat16),
            pltpu.VMEM((11, heads, 2, rows, HD), jnp.bfloat16),
            pltpu.VMEM((depth, width), jnp.bfloat16),
            pltpu.VMEM((heads, rows, HD), jnp.float32),
            pltpu.VMEM((heads, rows, HD), jnp.float32),
            pltpu.VMEM((heads, rows, HD), jnp.float32),
            pltpu.VMEM((heads, rows // 2, HD), jnp.bfloat16),
            pltpu.VMEM((2, heads, rows // 2, HD), jnp.bfloat16),
            pltpu.SemaphoreType.DMA((3, heads)),
            pltpu.SemaphoreType.DMA,
            pltpu.SemaphoreType.DMA((13, heads)),
            pltpu.SemaphoreType.DMA((11, heads)),
            pltpu.SemaphoreType.DMA((heads,)),
            pltpu.SemaphoreType.DMA((heads,)),
        ],
        compiler_params=pltpu.CompilerParams(
            collective_id=0, has_side_effects=True, vmem_limit_bytes=56 * 1024 * 1024
        ),
    )(query_states, key_states, value_states, out_weight)


def solution(mesh):
    in_specs = (
        P(("parts", "tm"), None, None),
        P(("parts", "tm"), None, None),
        P(("parts", "tm"), None, None),
        P(),
    )
    out_specs = P(("parts", "tm"), None)
    return jax.shard_map(
        per_device, mesh=mesh, in_specs=in_specs, out_specs=out_specs, check_vma=False
    )
```

profile of v0, /device:TPU:5, one launch (start us, length us, event | category | flops | bytes accessed | tf_op | source)
XLA Modules:
  0.0 84.3 jit_solution(7690222524487722975)
XLA Ops:
  0.0 81.9 %shard_map.46 = bf16[192,3072]{1,0:T(8,128)(2,1)} custom-call(bf16[1,384,768]{2,1,0:T(8,128)(2,1)} %q_hbm.1, bf16[1,384,768]{2,1,0:T(8,128)(2,1)} %k_hbm.1, bf16[1,384,768]{2,1,0:T(8,128)(2,1)} %v_hbm.1, bf16[1536,3072]{1,0:T(8,128)(2,1)} %w_hbm.1), custom_call_target="tpu_custom_call" | custom-call | tf_op jit(solution)/shard_map/pallas_call | solution.py:327
  81.9 2.4 %copy.6 = bf16[192,3072]{1,0:T(8,128)(2,1)} copy(bf16[192,3072]{1,0:T(8,128)(2,1)} %shard_map.46) | data formatting | bytes 2359296
where the time goes:
time: 84.4 us; the launch traced here: 84.3 us
  Pallas kernels  81.9 us (97%)
  local copies, waits for them, and re-layouts  2.36 us (3%)
    pallas_call x1, Pallas kernels, per_device(): pl.pallas_call(functools.partial(kernel, time_count, heads), out_shape=ja...  81.9 us
    unnamed x1, local copies, waits for them, and re-layouts  2.36 us

commit v1 on v0

--- a/solution.py
+++ b/solution.py
@@ -24,7 +24,7 @@
     return (time_step + 1) * 3 + col_step + 1
 
 
-def kernel(
+def general_kernel(
     time_count,
     heads,
     q_hbm,
@@ -319,13 +319,432 @@
                 )
 
 
-def per_device(query_states, key_states, value_states, out_weight):
+def balanced_kernel(
+    tiles,
+    q_hbm,
+    k_hbm,
+    v_hbm,
+    w_hbm,
+    out_ref,
+    q_s,
+    guest_q,
+    kv,
+    w_s,
+    m_s,
+    l_s,
+    acc_s,
+    mixed_s,
+    done_s,
+    other_s,
+    share_out,
+    share_in,
+    stat_out,
+    stat_in,
+    load_sem,
+    w_sem,
+    send_sem,
+    recv_sem,
+    q_send_sem,
+    q_recv_sem,
+    share_send_sem,
+    share_recv_sem,
+    att_send_sem,
+    att_recv_sem,
+):
+    heads, rows = q_s.shape[:2]
+    half = rows // 2
+    last = heads - 1
+    me = lax.axis_index("tm")
+    group = lax.rem(me, 2)
+    tile = lax.div(me, 2)
+    lower = tile < tiles // 2
+    role = jnp.where(lower, tile, tiles - 1 - tile)
+    side = lax.rem(role, 2)
+    is_cut_row = role >= 2
+    is_outer_row = jnp.logical_not(is_cut_row)
+    is_corner = role == 1
+    is_host = role == 3
+    pal = role + 1 - 2 * side
+    row_base = role - side
+    swapped = 5 - side
+    straight = 4 + side
+    far = 6 + side
+    pal_far = 7 - side
+    other_core = me + 1 - 2 * group
+
+    def device_of(slot):
+        return 2 * jnp.where(lower, slot, tiles - 1 - slot) + group
+
+    pal_device = device_of(pal)
+    up_down_device = device_of(jnp.where(is_cut_row, role - 2, role + 2))
+    cut_device = device_of(role + 2)
+
+    def load(h):
+        columns = pl.ds(pl.multiple_of(h * HD, HD), HD)
+        return (
+            pltpu.make_async_copy(k_hbm.at[0, :, columns], kv.at[role, h, 0], load_sem.at[0, h]),
+            pltpu.make_async_copy(v_hbm.at[0, :, columns], kv.at[role, h, 1], load_sem.at[1, h]),
+            pltpu.make_async_copy(q_hbm.at[0, :, columns], q_s.at[h], load_sem.at[2, h]),
+        )
+
+    def load_w(h, which):
+        owner = group if which == 0 else 1 - group
+        source = pl.ds(pl.multiple_of((owner * heads + h) * HD, HD), HD)
+        target = pl.ds(pl.multiple_of((2 * h + which) * HD, HD), HD)
+        return pltpu.make_async_copy(w_hbm.at[source], w_s.at[target], w_sem.at[h, which])
+
+    for h in (last, *range(last)):
+        for copy in load(jnp.int32(h)):
+            copy.start()
+
+    barrier = pltpu.get_barrier_semaphore()
+
+    def greet(device):
+        pl.semaphore_signal(barrier, inc=1, device_id={"tm": device}, device_id_type=MESH)
+
+    greet(other_core)
+    greet(pal_device)
+    greet(up_down_device)
+    pl.when(is_cut_row)(lambda: greet(cut_device))
+    pl.semaphore_wait(barrier, 3 + is_cut_row.astype(jnp.int32))
+
+    def transfer(way, slot, h, target, device):
+        return pltpu.make_async_remote_copy(
+            src_ref=kv.at[slot, h],
+            dst_ref=kv.at[target, h],
+            send_sem=send_sem.at[way, slot, h],
+            recv_sem=recv_sem.at[target, h],
+            device_id={"tm": device},
+            device_id_type=MESH,
+        )
+
+    def arrive(slot, h):
+        transfer(0, slot, h, slot, pal_device).wait_recv()
+
+    def to_pal(slot, h):
+        return transfer(0, slot, h, slot, pal_device)
+
+    def up_down(slot, h):
+        return transfer(1, slot, h, slot, up_down_device)
+
+    def cross(slot, h):
+        return transfer(1, slot, h, tiles - 1 - slot, cut_device)
+
+    def send_q(h):
+        return pltpu.make_async_remote_copy(
+            src_ref=q_s.at[h],
+            dst_ref=guest_q.at[h],
+            send_sem=q_send_sem.at[h],
+            recv_sem=q_recv_sem.at[h],
+            device_id={"tm": up_down_device},
+            device_id_type=MESH,
+        )
+
+    def send_share(h):
+        return tuple(
+            pltpu.make_async_remote_copy(
+                src_ref=source.at[h],
+                dst_ref=target.at[h],
+                send_sem=share_send_sem.at[which, h],
+                recv_sem=share_recv_sem.at[which, h],
+                device_id={"tm": up_down_device},
+                device_id_type=MESH,
+            )
+            for which, (source, target) in enumerate(((share_out, share_in), (stat_out, stat_in)))
+        )
+
+    own_half = pl.ds(pl.multiple_of(group * half, 16), half)
+    their_half = pl.ds(pl.multiple_of((1 - group) * half, 16), half)
+
+    def send_att(h):
+        return pltpu.make_async_remote_copy(
+            src_ref=done_s.at[h, their_half],
+            dst_ref=other_s.at[h],
+            send_sem=att_send_sem.at[h],
+            recv_sem=att_recv_sem.at[h],
+            device_id={"tm": other_core},
+            device_id_type=MESH,
+        )
+
+    def send_own(h):
+        to_pal(role, h).start()
+        pl.when(is_outer_row)(lambda: up_down(role, h).start())
+
+    for h in (last, *range(last)):
+        for copy in load(jnp.int32(h)):
+            copy.wait()
+        if h == last:
+            pl.when(is_cut_row)(lambda: cross(role, jnp.int32(last)).start())
+        else:
+            send_own(jnp.int32(h))
+    send_own(jnp.int32(last))
+    for h in range(heads):
+        pl.when(is_corner)(lambda: send_q(jnp.int32(h)).start())
+    for h in range(heads):
+        for which in range(2):
+            load_w(h, which).start()
+
+    exponent_scale = (HD ** (-0.5)) * LOG2E
+
+    def attend(queries, slots, h, old_max=None):
+        scores = [
+            lax.dot_general(queries, kv[slot, h, 0], (((1,), (1,)), ((), ())), preferred_element_type=jnp.float32)
+            for slot in slots
+        ]
+        row_max = functools.reduce(jnp.maximum, [jnp.max(s, axis=1, keepdims=True) for s in scores])
+        if old_max is not None:
+            row_max = jnp.maximum(row_max, old_max)
+        weights = [jnp.exp2((s - row_max) * exponent_scale) for s in scores]
+        total = sum(jnp.sum(w, axis=1, keepdims=True) for w in weights)
+        result = sum(
+            jnp.dot(w.astype(jnp.bfloat16), kv[slot, h, 1], preferred_element_type=jnp.float32)
+            for w, slot in zip(weights, slots)
+        )
+        return row_max, total, result
+
+    def attend_more(slots, h):
+        old_max = m_s[h][:, :1]
+        row_max, total, result = attend(q_s[h], slots, h, old_max)
+        keep = jnp.exp2((old_max - row_max) * exponent_scale)
+        return row_max, total + keep * l_s[h][:, :1], result + keep * acc_s[h]
+
+    def hold(h, row_max, total, result):
+        m_s[h] = jnp.broadcast_to(row_max, (rows, HD))
+        l_s[h] = jnp.broadcast_to(total, (rows, HD))
+        acc_s[h] = result
+
+    def finish(h, row_max, total, result):
+        done_s[h] = (result / total).astype(jnp.bfloat16)
+
+    def share(h):
+        row_max, total, result = attend(guest_q[h], (2, 6), h)
+        share_out[h] = (result / total).astype(jnp.bfloat16)
+        lane = lax.broadcasted_iota(jnp.int32, (rows, HD), 1)
+        stats = jnp.where(lax.rem(lane, 8) < 4, row_max, total)
+        stat_out[h] = jnp.transpose(stats)[:8]
+
+    def merge(h):
+        row_max, total, result = m_s[h], l_s[h], acc_s[h]
+        their_max = jnp.transpose(jnp.broadcast_to(stat_in[h, 0:1, :], (HD, rows)))
+        their_total = jnp.transpose(jnp.broadcast_to(stat_in[h, 4:5, :], (HD, rows)))
+        top = jnp.maximum(row_max, their_max)
+        keep = jnp.exp2((row_max - top) * exponent_scale)
+        weight = their_total * jnp.exp2((their_max - top) * exponent_scale)
+        finish(h, None, keep * total + weight, keep * result + weight * share_in[h].astype(jnp.float32))
+
+    width = out_ref.shape[1]
+    chunk = 512
+
+    def mix(first, stop):
+        lhs = jnp.concatenate(
+            [part for h in range(first, stop) for part in (done_s[h, own_half, :], other_s[h])], axis=1
+        )
+        depth = slice(2 * first * HD, 2 * stop * HD)
+
+        def product(n):
+            columns = pl.ds(n * chunk, chunk)
+            return columns, jnp.dot(lhs, w_s[depth, columns], preferred_element_type=jnp.float32)
+
+        return (product(n) for n in range(width // chunk))
+
+    early_heads = heads - 2
+
+    def ready(h):
+        return jnp.logical_and(h >= 0, h < heads)
+
+    @pl.loop(0, 2 * heads + 2)
+    def _(i):
+        settled = i - heads - jnp.where(is_cut_row, 2, 3)
+        pl.when(ready(settled))(lambda: send_att(settled).start())
+
+        @pl.when(i == 2 * heads)
+        def _():
+            for h in range(heads):
+                for which in range(2):
+                    load_w(h, which).wait()
+            for h in range(early_heads):
+                send_att(h).wait_recv()
+            for columns, value in mix(0, early_heads):
+                mixed_s[:, columns] = value
+
+        @pl.when(i < heads)
+        def _():
+            arrive(pal, i)
+            pl.when(role == 0)(lambda: up_down(pal, i).start())
+            pl.when(jnp.logical_and(is_cut_row, i < last))(lambda: cross(pal, i).start())
+
+        @pl.when(is_cut_row)
+        def _():
+            @pl.when(i == 0)
+            def _():
+                arrive(side, i)
+                cross(side, i).start()
+                arrive(straight, jnp.int32(last))
+                up_down(straight, jnp.int32(last)).start()
+                pl.when(is_host)(lambda: to_pal(straight, jnp.int32(last)).start())
+
+            relayed = i - 2
+
+            @pl.when(jnp.logical_and(relayed >= 0, relayed < last))
+            def _():
+                arrive(swapped, relayed)
+                up_down(swapped, relayed).start()
+
+            crossed = jnp.where(i == 2, 0, i - heads)
+
+            @pl.when(jnp.logical_or(i == 2, jnp.logical_and(crossed >= 1, crossed < heads)))
+            def _():
+                arrive(far, crossed)
+                to_pal(far, crossed).start()
+
+            def pass_on(h, first):
+                @pl.when(jnp.logical_and(h >= first, h < heads))
+                def _():
+                    arrive(side, h)
+                    cross(side, h).start()
+
+            pass_on(jnp.where(i == heads - 2, 1, 2 * (i - heads) + 4), 1)
+            pass_on(2 * (i - heads) + 5, 2)
+
+        @pl.when(is_outer_row)
+        def _():
+            @pl.when(i == 1)
+            def _():
+                arrive(straight, jnp.int32(last))
+                to_pal(straight, jnp.int32(last)).start()
+
+            relayed = i - 3
+
+            @pl.when(jnp.logical_and(relayed >= 0, relayed < last))
+            def _():
+                arrive(swapped, relayed)
+                to_pal(swapped, relayed).start()
+
+        @pl.when(i < heads)
+        def _():
+            hold(i, *attend(q_s[i], (row_base, row_base + 1), i))
+
+        @pl.when(is_outer_row)
+        def _():
+            h = jnp.where(i == heads, last, i - heads - 1)
+
+            @pl.when(jnp.logical_and(i >= heads, i < 2 * heads))
+            def _():
+                arrive(jnp.where(h == last, swapped, straight), h)
+                hold(h, *attend_more((4, 5), h))
+
+            ending = i - heads - 2
+
+            @pl.when(jnp.logical_and(ready(ending), role == 0))
+            def _():
+                finish(ending, None, l_s[ending], acc_s[ending])
+
+            @pl.when(jnp.logical_and(ready(ending), is_corner))
+            def _():
+                for copy in send_share(ending):
+                    copy.wait_recv()
+                merge(ending)
+
+        ending = i - heads - 1
+
+        @pl.when(jnp.logical_and(ready(ending), role == 2))
+        def _():
+            arrive(1, ending)
+            pl.when(ending == last)(lambda: arrive(5, ending))
+            arrive(pal_far, ending)
+            finish(ending, *attend_more((1, 5, 6, 7), ending))
+
+        @pl.when(jnp.logical_and(ready(ending), is_host))
+        def _():
+            send_q(ending).wait_recv()
+            arrive(pal_far, ending)
+            share(ending)
+            for copy in send_share(ending):
+                copy.start()
+            finish(ending, *attend_more((6, 7), ending))
+
+    pl.when(is_outer_row)(lambda: send_att(last).start())
+    for h in range(early_heads, heads):
+        send_att(h).wait_recv()
+    for columns, value in mix(early_heads, heads):
+        out_ref[:, columns] = (mixed_s[:, columns] + value).astype(out_ref.dtype)
+
+    @pl.loop(0, heads)
+    def _(h):
+        send_att(h).wait_send()
+        to_pal(role, h).wait_send()
+
+        @pl.when(is_cut_row)
+        def _():
+            to_pal(far, h).wait_send()
+            pl.when(jnp.logical_and(is_host, h == last))(lambda: to_pal(straight, h).wait_send())
+            up_down(jnp.where(h == last, straight, swapped), h).wait_send()
+            cross(jnp.where(h == last, role, pal), h).wait_send()
+            cross(side, h).wait_send()
+
+            @pl.when(is_host)
+            def _():
+                for copy in send_share(h):
+                    copy.wait_send()
+
+        @pl.when(is_outer_row)
+        def _():
+            to_pal(jnp.where(h == last, straight, swapped), h).wait_send()
+            up_down(role, h).wait_send()
+            pl.when(role == 0)(lambda: up_down(pal, h).wait_send())
+            pl.when(is_corner)(lambda: send_q(h).wait_send())
+
+
+def balanced_call(query_states, key_states, value_states, out_weight):
+    rows, half_width = query_states.shape[1:]
+    heads = half_width // HD
+    depth, width = out_weight.shape
+    tiles = lax.axis_size("tm") // 2
+    dma = pltpu.SemaphoreType.DMA
+    return pl.pallas_call(
+        functools.partial(balanced_kernel, tiles),
+        out_shape=jax.ShapeDtypeStruct((rows // 2, width), jnp.bfloat16),
+        in_specs=[pl.BlockSpec(memory_space=pl.ANY)] * 4,
+        out_specs=pl.BlockSpec(memory_space=pltpu.VMEM),
+        scratch_shapes=[
+            pltpu.VMEM((heads, rows, HD), jnp.bfloat16),
+            pltpu.VMEM((heads, rows, HD), jnp.bfloat16),
+            pltpu.VMEM((tiles, heads, 2, rows, HD), jnp.bfloat16),
+            pltpu.VMEM((depth, width), jnp.bfloat16),
+            pltpu.VMEM((heads, rows, HD), jnp.float32),
+            pltpu.VMEM((heads, rows, HD), jnp.float32),
+            pltpu.VMEM((heads, rows, HD), jnp.float32),
+            pltpu.VMEM((rows // 2, width), jnp.float32),
+            pltpu.VMEM((heads, rows, HD), jnp.bfloat16),
+            pltpu.VMEM((heads, rows // 2, HD), jnp.bfloat16),
+            pltpu.VMEM((heads, rows, HD), jnp.bfloat16),
+            pltpu.VMEM((heads, rows, HD), jnp.bfloat16),
+            pltpu.VMEM((heads, 8, rows), jnp.float32),
+            pltpu.VMEM((heads, 8, rows), jnp.float32),
+            dma((3, heads)),
+            dma((heads, 2)),
+            dma((2, tiles, heads)),
+            dma((tiles, heads)),
+            dma((heads,)),
+            dma((heads,)),
+            dma((2, heads)),
+            dma((2, heads)),
+            dma((heads,)),
+            dma((heads,)),
+        ],
+        compiler_params=pltpu.CompilerParams(
+            collective_id=0, has_side_effects=True, vmem_limit_bytes=56 * 1024 * 1024
+        ),
+    )(query_states, key_states, value_states, out_weight)
+
+
+def general_call(query_states, key_states, value_states, out_weight):
     rows, half_width = query_states.shape[1:]
     heads = half_width // HD
     depth, width = out_weight.shape
     time_count = lax.axis_size("tm") // (2 * TCOLS)
     return pl.pallas_call(
-        functools.partial(kernel, time_count, heads),
+        functools.partial(general_kernel, time_count, heads),
         out_shape=jax.ShapeDtypeStruct((rows // 2, width), jnp.bfloat16),
         in_specs=[pl.BlockSpec(memory_space=pl.ANY)] * 4,
         out_specs=pl.BlockSpec(memory_space=pltpu.VMEM),
@@ -351,6 +770,11 @@
     )(query_states, key_states, value_states, out_weight)
 
 
+def per_device(query_states, key_states, value_states, out_weight):
+    call = balanced_call if lax.axis_size("tm") == 4 * TCOLS else general_call
+    return call(query_states, key_states, value_states, out_weight)
+
+
 def solution(mesh):
     in_specs = (
         P(("parts", "tm"), None, None),

time: 84.4 us -> 74.6 us (0.88)
  Pallas kernels: 81.9 us -> 72 us
    pallas_call x1, Pallas kernels: 81.9 us -> 72 us  [balanced_call(): pl.pallas_call(functools.partial(balanced_kernel, tiles), out_shape=jax.S...]
where the time goes in v1:
time: 74.6 us; the launch traced here: 74.4 us
  Pallas kernels  72 us (97%)
  local copies, waits for them, and re-layouts  2.36 us (3%)
    pallas_call x1, Pallas kernels, balanced_call(): pl.pallas_call(functools.partial(balanced_kernel, tiles), out_shape=jax.S...  72 us
    unnamed x1, local copies, waits for them, and re-layouts  2.36 us

profile of v1, /device:TPU:5, one launch (start us, length us, event | category | flops | bytes accessed | tf_op | source)
XLA Modules:
  0.0 74.4 jit_solution(1419903430530765804)
XLA Ops:
  0.0 72.0 %shard_map.46 = bf16[192,3072]{1,0:T(8,128)(2,1)} custom-call(bf16[1,384,768]{2,1,0:T(8,128)(2,1)} %q_hbm.1, bf16[1,384,768]{2,1,0:T(8,128)(2,1)} %k_hbm.1, bf16[1,384,768]{2,1,0:T(8,128)(2,1)} %v_hbm.1, bf16[1536,3072]{1,0:T(8,128)(2,1)} %w_hbm.1), custom_call_target="tpu_custom_call" | custom-call | tf_op jit(solution)/shard_map/pallas_call | solution.py:704
  72.0 2.4 %copy.6 = bf16[192,3072]{1,0:T(8,128)(2,1)} copy(bf16[192,3072]{1,0:T(8,128)(2,1)} %shard_map.46) | data formatting | bytes 2359296

commit v2 on v1

--- a/solution.py
+++ b/solution.py
@@ -733,9 +733,9 @@
             dma((heads,)),
         ],
         compiler_params=pltpu.CompilerParams(
-            collective_id=0, has_side_effects=True, vmem_limit_bytes=56 * 1024 * 1024
+            collective_id=0, has_side_effects=True, vmem_limit_bytes=40 * 1024 * 1024
         ),
-    )(query_states, key_states, value_states, out_weight)
+    )(*(pltpu.with_memory_space_constraint(x, pltpu.HBM) for x in (query_states, key_states, value_states, out_weight)))
 
 
 def general_call(query_states, key_states, value_states, out_weight):

time: 74.6 us -> 72.2 us (0.968)
  local copies, waits for them, and re-layouts: 2.36 us -> 1.02 us
  Pallas kernels: 72 us -> 71 us
    unnamed x1, local copies, waits for them, and re-layouts: 2.36 us -> 1.02 us
    pallas_call x1, Pallas kernels: 72 us -> 71 us  [balanced_call(): pl.pallas_call(functools.partial(balanced_kernel, tiles), out_shape=jax.S...]
where the time goes in v2:
time: 72.2 us; the launch traced here: 72 us
  Pallas kernels  71 us (98%)
  local copies, waits for them, and re-layouts  1.02 us (1%)
    pallas_call x1, Pallas kernels, balanced_call(): pl.pallas_call(functools.partial(balanced_kernel, tiles), out_shape=jax.S...  71 us

profile of v2, /device:TPU:5, one launch (start us, length us, event | category | flops | bytes accessed | tf_op | source)
XLA Modules:
  0.0 72.0 jit_solution(11240328965226356080)
XLA Ops:
  0.0 71.0 %shard_map.46 = bf16[192,3072]{1,0:T(8,128)(2,1)S(1)} custom-call(bf16[1,384,768]{2,1,0:T(8,128)(2,1)} %q_hbm.1, bf16[1,384,768]{2,1,0:T(8,128)(2,1)} %k_hbm.1, bf16[1,384,768]{2,1,0:T(8,128)(2,1)} %v_hbm.1, bf16[1536,3072]{1,0:T(8,128)(2,1)} %w_hbm.1), custom_call_target="tpu_custom_call" | custom-call | tf_op jit(solution)/shard_map/pallas_call | solution.py:704
  71.0 1.0 %copy.6 = bf16[192,3072]{1,0:T(8,128)(2,1)} copy(bf16[192,3072]{1,0:T(8,128)(2,1)S(1)} %shard_map.46) | data formatting | bytes 2359296

commit v3 on v2

--- a/solution.py
+++ b/solution.py
@@ -18,6 +18,10 @@
 LAG_TIME = 2
 LAG_CORNER = 3
 LAG_MIDDLE = 5
+
+NEAR = 2
+OUT_CHUNK = 512
+FIRST_OWN, FIRST_CROSSED, LAST_CROSSED, LAST_FAR = range(4)
 
 
 def slot_of(time_step, col_step):
@@ -341,6 +345,7 @@
     stat_out,
     stat_in,
     load_sem,
+    q_sem,
     w_sem,
     send_sem,
     recv_sem,
@@ -354,6 +359,7 @@
     heads, rows = q_s.shape[:2]
     half = rows // 2
     last = heads - 1
+    early_heads = heads - 2
     me = lax.axis_index("tm")
     group = lax.rem(me, 2)
     tile = lax.div(me, 2)
@@ -363,6 +369,7 @@
     is_cut_row = role >= 2
     is_outer_row = jnp.logical_not(is_cut_row)
     is_corner = role == 1
+    is_near = role == 2
     is_host = role == 3
     pal = role + 1 - 2 * side
     row_base = role - side
@@ -378,20 +385,21 @@
     pal_device = device_of(pal)
     up_down_device = device_of(jnp.where(is_cut_row, role - 2, role + 2))
     cut_device = device_of(role + 2)
+    corner_device = device_of(1)
 
     def load(h):
         columns = pl.ds(pl.multiple_of(h * HD, HD), HD)
         return (
-            pltpu.make_async_copy(k_hbm.at[0, :, columns], kv.at[role, h, 0], load_sem.at[0, h]),
-            pltpu.make_async_copy(v_hbm.at[0, :, columns], kv.at[role, h, 1], load_sem.at[1, h]),
-            pltpu.make_async_copy(q_hbm.at[0, :, columns], q_s.at[h], load_sem.at[2, h]),
+            pltpu.make_async_copy(k_hbm.at[0, :, columns], kv.at[role, h, 0], load_sem.at[h]),
+            pltpu.make_async_copy(v_hbm.at[0, :, columns], kv.at[role, h, 1], load_sem.at[h]),
+            pltpu.make_async_copy(q_hbm.at[0, :, columns], q_s.at[h], q_sem),
         )
 
     def load_w(h, which):
         owner = group if which == 0 else 1 - group
         source = pl.ds(pl.multiple_of((owner * heads + h) * HD, HD), HD)
         target = pl.ds(pl.multiple_of((2 * h + which) * HD, HD), HD)
-        return pltpu.make_async_copy(w_hbm.at[source], w_s.at[target], w_sem.at[h, which])
+        return pltpu.make_async_copy(w_hbm.at[source], w_s.at[target], w_sem)
 
     for h in (last, *range(last)):
         for copy in load(jnp.int32(h)):
@@ -406,37 +414,46 @@
     greet(pal_device)
     greet(up_down_device)
     pl.when(is_cut_row)(lambda: greet(cut_device))
-    pl.semaphore_wait(barrier, 3 + is_cut_row.astype(jnp.int32))
-
-    def transfer(way, slot, h, target, device):
+    pl.when(is_corner)(lambda: greet(device_of(2)))
+    pl.semaphore_wait(barrier, 3 + is_cut_row.astype(jnp.int32) + is_near.astype(jnp.int32))
+
+    def transfer(way, slot, h, target, device, part=None, kind=0, landing=0):
         return pltpu.make_async_remote_copy(
-            src_ref=kv.at[slot, h],
-            dst_ref=kv.at[target, h],
-            send_sem=send_sem.at[way, slot, h],
-            recv_sem=recv_sem.at[target, h],
+            src_ref=kv.at[slot, h] if part is None else kv.at[slot, h, part],
+            dst_ref=kv.at[target, h] if part is None else kv.at[target, h, part],
+            send_sem=send_sem.at[way],
+            recv_sem=recv_sem.at[landing, kind] if part == 1 else recv_sem.at[target, h],
             device_id={"tm": device},
             device_id_type=MESH,
         )
 
-    def arrive(slot, h):
-        transfer(0, slot, h, slot, pal_device).wait_recv()
-
-    def to_pal(slot, h):
-        return transfer(0, slot, h, slot, pal_device)
+    def arrive(slot, h, part=None, kind=0):
+        transfer(0, slot, h, slot, pal_device, part, kind, role).wait_recv()
+
+    def to_pal(slot, h, part=None, kind=0, way=0):
+        return transfer(way, slot, h, slot, pal_device, part, kind, pal)
 
     def up_down(slot, h):
         return transfer(1, slot, h, slot, up_down_device)
 
-    def cross(slot, h):
-        return transfer(1, slot, h, tiles - 1 - slot, cut_device)
-
-    def send_q(h):
+    def cross(slot, h, part=None, kind=0):
+        return transfer(2, slot, h, tiles - 1 - slot, cut_device, part, kind, pal)
+
+    def split_or_whole(is_split, act):
+        pl.when(jnp.logical_not(is_split))(lambda: act(None))
+
+        @pl.when(is_split)
+        def _():
+            for part in range(2):
+                act(part)
+
+    def send_q(h, source=q_s, device=up_down_device):
         return pltpu.make_async_remote_copy(
-            src_ref=q_s.at[h],
+            src_ref=source.at[h],
             dst_ref=guest_q.at[h],
-            send_sem=q_send_sem.at[h],
+            send_sem=q_send_sem,
             recv_sem=q_recv_sem.at[h],
-            device_id={"tm": up_down_device},
+            device_id={"tm": device},
             device_id_type=MESH,
         )
 
@@ -445,9 +462,9 @@
             pltpu.make_async_remote_copy(
                 src_ref=source.at[h],
                 dst_ref=target.at[h],
-                send_sem=share_send_sem.at[which, h],
+                send_sem=share_send_sem.at[which],
                 recv_sem=share_recv_sem.at[which, h],
-                device_id={"tm": up_down_device},
+                device_id={"tm": corner_device},
                 device_id_type=MESH,
             )
             for which, (source, target) in enumerate(((share_out, share_in), (stat_out, stat_in)))
@@ -460,29 +477,42 @@
         return pltpu.make_async_remote_copy(
             src_ref=done_s.at[h, their_half],
             dst_ref=other_s.at[h],
-            send_sem=att_send_sem.at[h],
-            recv_sem=att_recv_sem.at[h],
+            send_sem=att_send_sem,
+            recv_sem=att_recv_sem.at[jnp.where(h < early_heads, 0, 1)],
             device_id={"tm": other_core},
             device_id_type=MESH,
         )
 
+    def recv_att(first, stop, which):
+        rows_in = other_s.at[pl.ds(first, stop - first)]
+        pltpu.make_async_copy(rows_in, rows_in, att_recv_sem.at[which]).wait()
+
     def send_own(h):
-        to_pal(role, h).start()
+        if h == 0:
+            split_or_whole(is_cut_row, lambda part: to_pal(role, 0, part, FIRST_OWN).start())
+        else:
+            to_pal(role, h).start()
         pl.when(is_outer_row)(lambda: up_down(role, h).start())
 
     for h in (last, *range(last)):
-        for copy in load(jnp.int32(h)):
-            copy.wait()
+        pltpu.make_async_copy(kv.at[role, h], kv.at[role, h], load_sem.at[h]).wait()
         if h == last:
-            pl.when(is_cut_row)(lambda: cross(role, jnp.int32(last)).start())
+            pl.when(is_cut_row)(lambda: cross(role, last).start())
         else:
-            send_own(jnp.int32(h))
-    send_own(jnp.int32(last))
-    for h in range(heads):
-        pl.when(is_corner)(lambda: send_q(jnp.int32(h)).start())
-    for h in range(heads):
-        for which in range(2):
-            load_w(h, which).start()
+            send_own(h)
+        if h == 1:
+            pltpu.make_async_copy(q_s, q_s, q_sem).wait()
+
+            @pl.when(is_corner)
+            def _():
+                for near in range(heads - NEAR, heads):
+                    send_q(near, device=pal_device).start()
+    send_own(last)
+
+    @pl.when(is_corner)
+    def _():
+        for h in range(heads - NEAR):
+            send_q(h).start()
 
     exponent_scale = (HD ** (-0.5)) * LOG2E
 
@@ -533,7 +563,7 @@
         finish(h, None, keep * total + weight, keep * result + weight * share_in[h].astype(jnp.float32))
 
     width = out_ref.shape[1]
-    chunk = 512
+    chunk = OUT_CHUNK
 
     def mix(first, stop):
         lhs = jnp.concatenate(
@@ -546,8 +576,6 @@
             return columns, jnp.dot(lhs, w_s[depth, columns], preferred_element_type=jnp.float32)
 
         return (product(n) for n in range(width // chunk))
-
-    early_heads = heads - 2
 
     def ready(h):
         return jnp.logical_and(h >= 0, h < heads)
@@ -557,17 +585,7 @@
         settled = i - heads - jnp.where(is_cut_row, 2, 3)
         pl.when(ready(settled))(lambda: send_att(settled).start())
 
-        @pl.when(i == 2 * heads)
-        def _():
-            for h in range(heads):
-                for which in range(2):
-                    load_w(h, which).wait()
-            for h in range(early_heads):
-                send_att(h).wait_recv()
-            for columns, value in mix(0, early_heads):
-                mixed_s[:, columns] = value
-
-        @pl.when(i < heads)
+        @pl.when(jnp.logical_and(i < heads, jnp.logical_or(is_outer_row, i > 0)))
         def _():
             arrive(pal, i)
             pl.when(role == 0)(lambda: up_down(pal, i).start())
@@ -577,31 +595,45 @@
         def _():
             @pl.when(i == 0)
             def _():
-                arrive(side, i)
-                cross(side, i).start()
-                arrive(straight, jnp.int32(last))
-                up_down(straight, jnp.int32(last)).start()
-                pl.when(is_host)(lambda: to_pal(straight, jnp.int32(last)).start())
+                for part in range(2):
+                    arrive(pal, 0, part, FIRST_OWN)
+                    cross(pal, 0, part, FIRST_CROSSED).start()
+                arrive(side, 0)
+                cross(side, 0).start()
+                arrive(straight, last)
+                up_down(straight, last).start()
+                pl.when(is_host)(lambda: to_pal(straight, last, way=3).start())
+
+            @pl.when(i == 2)
+            def _():
+                for part in range(2):
+                    arrive(swapped, 0, part, FIRST_CROSSED)
+                up_down(swapped, 0).start()
+                arrive(far, 0)
+                to_pal(far, 0).start()
 
             relayed = i - 2
 
-            @pl.when(jnp.logical_and(relayed >= 0, relayed < last))
+            @pl.when(jnp.logical_and(relayed >= 1, relayed < last))
             def _():
                 arrive(swapped, relayed)
                 up_down(swapped, relayed).start()
 
-            crossed = jnp.where(i == 2, 0, i - heads)
-
-            @pl.when(jnp.logical_or(i == 2, jnp.logical_and(crossed >= 1, crossed < heads)))
-            def _():
-                arrive(far, crossed)
-                to_pal(far, crossed).start()
+            crossed = i - heads
+
+            def hand_on(part):
+                arrive(far, crossed, part, LAST_CROSSED)
+                to_pal(far, crossed, part, LAST_FAR).start()
+
+            @pl.when(jnp.logical_and(crossed >= 1, crossed < heads))
+            def _():
+                split_or_whole(crossed == last, hand_on)
 
             def pass_on(h, first):
                 @pl.when(jnp.logical_and(h >= first, h < heads))
                 def _():
                     arrive(side, h)
-                    cross(side, h).start()
+                    split_or_whole(h == last, lambda part: cross(side, h, part, LAST_CROSSED).start())
 
             pass_on(jnp.where(i == heads - 2, 1, 2 * (i - heads) + 4), 1)
             pass_on(2 * (i - heads) + 5, 2)
@@ -610,8 +642,8 @@
         def _():
             @pl.when(i == 1)
             def _():
-                arrive(straight, jnp.int32(last))
-                to_pal(straight, jnp.int32(last)).start()
+                arrive(straight, last)
+                to_pal(straight, last).start()
 
             relayed = i - 3
 
@@ -620,9 +652,36 @@
                 arrive(swapped, relayed)
                 to_pal(swapped, relayed).start()
 
+        nearby = i - heads
+
+        @pl.when(jnp.logical_and(is_near, jnp.logical_and(nearby >= heads - NEAR, nearby < heads)))
+        def _():
+            send_q(nearby).wait_recv()
+            share(nearby)
+            for copy in send_share(nearby):
+                copy.start()
+
+        @pl.when(i == 2 * heads - jnp.where(jnp.logical_and(is_cut_row, group == 0), 1, 0))
+        def _():
+            pltpu.make_async_copy(w_hbm, w_s, w_sem).wait()
+            recv_att(0, early_heads, 0)
+            for columns, value in mix(0, early_heads):
+                mixed_s[:, columns] = value
+
+        @pl.when(jnp.logical_and(i >= 1, i <= heads))
+        def _():
+            for which in range(2):
+                load_w(i - 1, which).start()
+
         @pl.when(i < heads)
         def _():
             hold(i, *attend(q_s[i], (row_base, row_base + 1), i))
+
+        @pl.when(jnp.logical_and(role == 0, i == 2))
+        def _():
+            for h in range(heads - NEAR, heads):
+                send_q(h).wait_recv()
+                send_q(h, source=guest_q).start()
 
         @pl.when(is_outer_row)
         def _():
@@ -647,52 +706,64 @@
 
         ending = i - heads - 1
 
-        @pl.when(jnp.logical_and(ready(ending), role == 2))
+        @pl.when(jnp.logical_and(ready(ending), is_cut_row))
+        def _():
+            split_or_whole(ending == last, lambda part: arrive(pal_far, ending, part, LAST_FAR))
+
+        @pl.when(jnp.logical_and(ready(ending), is_near))
         def _():
             arrive(1, ending)
             pl.when(ending == last)(lambda: arrive(5, ending))
-            arrive(pal_far, ending)
             finish(ending, *attend_more((1, 5, 6, 7), ending))
 
         @pl.when(jnp.logical_and(ready(ending), is_host))
         def _():
-            send_q(ending).wait_recv()
-            arrive(pal_far, ending)
-            share(ending)
-            for copy in send_share(ending):
-                copy.start()
+            @pl.when(ending < heads - NEAR)
+            def _():
+                send_q(ending).wait_recv()
+                share(ending)
+                for copy in send_share(ending):
+                    copy.start()
+
             finish(ending, *attend_more((6, 7), ending))
 
     pl.when(is_outer_row)(lambda: send_att(last).start())
-    for h in range(early_heads, heads):
-        send_att(h).wait_recv()
+    recv_att(early_heads, heads, 1)
     for columns, value in mix(early_heads, heads):
         out_ref[:, columns] = (mixed_s[:, columns] + value).astype(out_ref.dtype)
 
-    @pl.loop(0, heads)
-    def _(h):
-        send_att(h).wait_send()
-        to_pal(role, h).wait_send()
-
-        @pl.when(is_cut_row)
-        def _():
-            to_pal(far, h).wait_send()
-            pl.when(jnp.logical_and(is_host, h == last))(lambda: to_pal(straight, h).wait_send())
-            up_down(jnp.where(h == last, straight, swapped), h).wait_send()
-            cross(jnp.where(h == last, role, pal), h).wait_send()
-            cross(side, h).wait_send()
-
-            @pl.when(is_host)
-            def _():
-                for copy in send_share(h):
-                    copy.wait_send()
-
-        @pl.when(is_outer_row)
-        def _():
-            to_pal(jnp.where(h == last, straight, swapped), h).wait_send()
-            up_down(role, h).wait_send()
-            pl.when(role == 0)(lambda: up_down(pal, h).wait_send())
-            pl.when(is_corner)(lambda: send_q(h).wait_send())
+    def drain(way, count):
+        tiles_sent = kv.at[pl.ds(0, count)]
+        pltpu.make_async_remote_copy(
+            src_ref=tiles_sent,
+            dst_ref=tiles_sent,
+            send_sem=send_sem.at[way],
+            recv_sem=recv_sem.at[0, 0],
+            device_id={"tm": pal_device},
+            device_id_type=MESH,
+        ).wait_send()
+
+    def drain_rows(sent, sem):
+        pltpu.make_async_remote_copy(
+            src_ref=sent,
+            dst_ref=sent,
+            send_sem=sem,
+            recv_sem=recv_sem.at[0, 0],
+            device_id={"tm": pal_device},
+            device_id_type=MESH,
+        ).wait_send()
+
+    drain(0, 2)
+    drain(1, 1)
+    drain_rows(other_s, att_send_sem)
+    pl.when(role == 0)(lambda: drain(1, 1))
+    pl.when(role == 0)(lambda: drain_rows(guest_q.at[pl.ds(0, NEAR)], q_send_sem))
+    pl.when(is_corner)(lambda: drain_rows(q_s, q_send_sem))
+    pl.when(is_cut_row)(lambda: drain(2, 2))
+    pl.when(is_host)(lambda: drain_rows(kv.at[0, 0], send_sem.at[3]))
+    for count, sender in ((heads - NEAR, is_host), (NEAR, is_near)):
+        pl.when(sender)(lambda count=count: drain_rows(share_out.at[pl.ds(0, count)], share_send_sem.at[0]))
+        pl.when(sender)(lambda count=count: drain_rows(stat_out.at[pl.ds(0, count)], share_send_sem.at[1]))
 
 
 def balanced_call(query_states, key_states, value_states, out_weight):
@@ -721,16 +792,17 @@
             pltpu.VMEM((heads, rows, HD), jnp.bfloat16),
             pltpu.VMEM((heads, 8, rows), jnp.float32),
             pltpu.VMEM((heads, 8, rows), jnp.float32),
-            dma((3, heads)),
-            dma((heads, 2)),
-            dma((2, tiles, heads)),
+            dma((heads,)),
+            dma,
+            dma,
+            dma((4,)),
             dma((tiles, heads)),
+            dma,
             dma((heads,)),
-            dma((heads,)),
+            dma((2,)),
             dma((2, heads)),
-            dma((2, heads)),
-            dma((heads,)),
-            dma((heads,)),
+            dma,
+            dma((2,)),
         ],
         compiler_params=pltpu.CompilerParams(
             collective_id=0, has_side_effects=True, vmem_limit_bytes=40 * 1024 * 1024

time: 72.2 us -> 67.1 us (0.929)
  the two profiles are of different devices: /device:TPU:5 before, /device:TPU:0 now
where the time goes in v3:
time: 67.1 us; the launch traced here: 66.9 us
  Pallas kernels  65.9 us (98%)
  local copies, waits for them, and re-layouts  1.02 us (2%)
    pallas_call x1, Pallas kernels, balanced_call(): pl.pallas_call(functools.partial(balanced_kernel, tiles), out_shape=jax.S...  65.9 us

profile of v3, /device:TPU:0, one launch (start us, length us, event | category | flops | bytes accessed | tf_op | source)
XLA Modules:
  0.0 66.9 jit_solution(12427910107793864599)
XLA Ops:
  0.0 65.9 %shard_map.46 = bf16[192,3072]{1,0:T(8,128)(2,1)S(1)} custom-call(bf16[1,384,768]{2,1,0:T(8,128)(2,1)} %q_hbm.1, bf16[1,384,768]{2,1,0:T(8,128)(2,1)} %k_hbm.1, bf16[1,384,768]{2,1,0:T(8,128)(2,1)} %v_hbm.1, bf16[1536,3072]{1,0:T(8,128)(2,1)} %w_hbm.1), custom_call_target="tpu_custom_call" | custom-call | tf_op jit(solution)/shard_map/pallas_call | solution.py:775
  65.9 1.0 %copy.6 = bf16[192,3072]{1,0:T(8,128)(2,1)} copy(bf16[192,3072]{1,0:T(8,128)(2,1)S(1)} %shard_map.46) | data formatting | bytes 2359296

commit v4 on v3

--- a/solution.py
+++ b/solution.py
@@ -21,7 +21,7 @@
 
 NEAR = 2
 OUT_CHUNK = 512
-FIRST_OWN, FIRST_CROSSED, LAST_CROSSED, LAST_FAR = range(4)
+FIRST_OWN, FIRST_CROSSED = range(2)
 
 
 def slot_of(time_step, col_step):
@@ -323,6 +323,12 @@
                 )
 
 
+def crossing_order(heads):
+    order = [(from_pal, h) for h in range(heads - 4) for from_pal in (True, False)]
+    order += [(True, heads - 4), (True, heads - 3), (False, heads - 4), (True, heads - 2)]
+    return order + [(False, h) for h in range(heads - 3, heads)]
+
+
 def balanced_kernel(
     tiles,
     q_hbm,
@@ -344,6 +350,11 @@
     share_in,
     stat_out,
     stat_in,
+    pal_q,
+    pal_share_out,
+    pal_share_in,
+    pal_stat_out,
+    pal_stat_in,
     load_sem,
     q_sem,
     w_sem,
@@ -353,13 +364,16 @@
     q_recv_sem,
     share_send_sem,
     share_recv_sem,
+    pal_send_sem,
+    pal_recv_sem,
     att_send_sem,
     att_recv_sem,
 ):
     heads, rows = q_s.shape[:2]
     half = rows // 2
     last = heads - 1
-    early_heads = heads - 2
+    early_heads = heads - 3
+    tail = heads - NEAR
     me = lax.axis_index("tm")
     group = lax.rem(me, 2)
     tile = lax.div(me, 2)
@@ -430,11 +444,11 @@
     def arrive(slot, h, part=None, kind=0):
         transfer(0, slot, h, slot, pal_device, part, kind, role).wait_recv()
 
-    def to_pal(slot, h, part=None, kind=0, way=0):
-        return transfer(way, slot, h, slot, pal_device, part, kind, pal)
-
-    def up_down(slot, h):
-        return transfer(1, slot, h, slot, up_down_device)
+    def to_pal(slot, h, part=None, kind=0):
+        return transfer(0, slot, h, slot, pal_device, part, kind, pal)
+
+    def up_down(slot, h, way=1):
+        return transfer(way, slot, h, slot, up_down_device)
 
     def cross(slot, h, part=None, kind=0):
         return transfer(2, slot, h, tiles - 1 - slot, cut_device, part, kind, pal)
@@ -457,17 +471,43 @@
             device_id_type=MESH,
         )
 
-    def send_share(h):
+    def lend_q(h):
+        return pltpu.make_async_remote_copy(
+            src_ref=q_s.at[h],
+            dst_ref=share_in.at[h],
+            send_sem=q_send_sem,
+            recv_sem=share_recv_sem.at[0, h],
+            device_id={"tm": up_down_device},
+            device_id_type=MESH,
+        )
+
+    def send_share(h, device=corner_device):
         return tuple(
             pltpu.make_async_remote_copy(
                 src_ref=source.at[h],
                 dst_ref=target.at[h],
                 send_sem=share_send_sem.at[which],
                 recv_sem=share_recv_sem.at[which, h],
-                device_id={"tm": corner_device},
+                device_id={"tm": device},
                 device_id_type=MESH,
             )
             for which, (source, target) in enumerate(((share_out, share_in), (stat_out, stat_in)))
+        )
+
+    def send_pal(source, target, which, index):
+        return pltpu.make_async_remote_copy(
+            src_ref=source,
+            dst_ref=target,
+            send_sem=pal_send_sem.at[which],
+            recv_sem=pal_recv_sem.at[which, index],
+            device_id={"tm": pal_device},
+            device_id_type=MESH,
+        )
+
+    def send_pal_share(index):
+        return (
+            send_pal(pal_share_out.at[index], pal_share_in.at[index], 1, index),
+            send_pal(pal_stat_out.at[index], pal_stat_in.at[index], 2, index),
         )
 
     own_half = pl.ds(pl.multiple_of(group * half, 16), half)
@@ -513,6 +553,16 @@
     def _():
         for h in range(heads - NEAR):
             send_q(h).start()
+
+    @pl.when(is_near)
+    def _():
+        for h in range(heads):
+            lend_q(h).start()
+
+    @pl.when(is_cut_row)
+    def _():
+        for h in range(tail, heads):
+            send_pal(q_s.at[h], pal_q.at[h - tail], 0, h - tail).start()
 
     exponent_scale = (HD ** (-0.5)) * LOG2E
 
@@ -546,21 +596,21 @@
     def finish(h, row_max, total, result):
         done_s[h] = (result / total).astype(jnp.bfloat16)
 
-    def share(h):
-        row_max, total, result = attend(guest_q[h], (2, 6), h)
-        share_out[h] = (result / total).astype(jnp.bfloat16)
+    def share(h, queries, slots, share_to, stat_to):
+        row_max, total, result = attend(queries, slots, h)
+        share_to[...] = (result / total).astype(jnp.bfloat16)
         lane = lax.broadcasted_iota(jnp.int32, (rows, HD), 1)
         stats = jnp.where(lax.rem(lane, 8) < 4, row_max, total)
-        stat_out[h] = jnp.transpose(stats)[:8]
-
-    def merge(h):
+        stat_to[...] = jnp.transpose(stats)[:8]
+
+    def merge(h, shared, stats):
         row_max, total, result = m_s[h], l_s[h], acc_s[h]
-        their_max = jnp.transpose(jnp.broadcast_to(stat_in[h, 0:1, :], (HD, rows)))
-        their_total = jnp.transpose(jnp.broadcast_to(stat_in[h, 4:5, :], (HD, rows)))
+        their_max = jnp.transpose(jnp.broadcast_to(stats[0:1, :], (HD, rows)))
+        their_total = jnp.transpose(jnp.broadcast_to(stats[4:5, :], (HD, rows)))
         top = jnp.maximum(row_max, their_max)
         keep = jnp.exp2((row_max - top) * exponent_scale)
         weight = their_total * jnp.exp2((their_max - top) * exponent_scale)
-        finish(h, None, keep * total + weight, keep * result + weight * share_in[h].astype(jnp.float32))
+        return top, keep * total + weight, keep * result + weight * shared[...].astype(jnp.float32)
 
     width = out_ref.shape[1]
     chunk = OUT_CHUNK
@@ -582,13 +632,15 @@
 
     @pl.loop(0, 2 * heads + 2)
     def _(i):
-        settled = i - heads - jnp.where(is_cut_row, 2, 3)
-        pl.when(ready(settled))(lambda: send_att(settled).start())
+        settled = jnp.where(
+            jnp.logical_and(role == 0, i == heads + 1), last, i - heads - jnp.where(is_corner, 3, 2)
+        )
+        settles = jnp.logical_and(ready(settled), jnp.logical_or(role != 0, i <= 2 * heads))
+        pl.when(settles)(lambda: send_att(settled).start())
 
         @pl.when(jnp.logical_and(i < heads, jnp.logical_or(is_outer_row, i > 0)))
         def _():
             arrive(pal, i)
-            pl.when(role == 0)(lambda: up_down(pal, i).start())
             pl.when(jnp.logical_and(is_cut_row, i < last))(lambda: cross(pal, i).start())
 
         @pl.when(is_cut_row)
@@ -602,41 +654,28 @@
                 cross(side, 0).start()
                 arrive(straight, last)
                 up_down(straight, last).start()
-                pl.when(is_host)(lambda: to_pal(straight, last, way=3).start())
-
-            @pl.when(i == 2)
-            def _():
-                for part in range(2):
-                    arrive(swapped, 0, part, FIRST_CROSSED)
-                up_down(swapped, 0).start()
-                arrive(far, 0)
-                to_pal(far, 0).start()
-
-            relayed = i - 2
-
-            @pl.when(jnp.logical_and(relayed >= 1, relayed < last))
-            def _():
-                arrive(swapped, relayed)
-                up_down(swapped, relayed).start()
-
-            crossed = i - heads
-
-            def hand_on(part):
-                arrive(far, crossed, part, LAST_CROSSED)
-                to_pal(far, crossed, part, LAST_FAR).start()
-
-            @pl.when(jnp.logical_and(crossed >= 1, crossed < heads))
-            def _():
-                split_or_whole(crossed == last, hand_on)
-
-            def pass_on(h, first):
-                @pl.when(jnp.logical_and(h >= first, h < heads))
-                def _():
-                    arrive(side, h)
-                    split_or_whole(h == last, lambda part: cross(side, h, part, LAST_CROSSED).start())
-
-            pass_on(jnp.where(i == heads - 2, 1, 2 * (i - heads) + 4), 1)
-            pass_on(2 * (i - heads) + 5, 2)
+
+            def pass_on(h):
+                arrive(side, h)
+                cross(side, h).start()
+
+            def take(from_pal, h):
+                if from_pal:
+                    for part in range(2) if h == 0 else (None,):
+                        arrive(swapped, h, part, FIRST_CROSSED)
+                    up_down(swapped, h).start()
+                else:
+                    arrive(far, h)
+                    if h < tail:
+                        to_pal(far, h).start()
+
+            at = 0
+            for place, (from_pal, h) in enumerate(crossing_order(heads)):
+                at = max(at, h)
+                if not from_pal and h > 0:
+                    pl.when(i == at)(lambda h=h: pass_on(h))
+            for place, (from_pal, h) in enumerate(crossing_order(heads)):
+                pl.when(i == place + 1)(lambda from_pal=from_pal, h=h: take(from_pal, h))
 
         @pl.when(is_outer_row)
         def _():
@@ -645,23 +684,33 @@
                 arrive(straight, last)
                 to_pal(straight, last).start()
 
-            relayed = i - 3
-
-            @pl.when(jnp.logical_and(relayed >= 0, relayed < last))
-            def _():
-                arrive(swapped, relayed)
-                to_pal(swapped, relayed).start()
+            def relay(j):
+                arrive(swapped, j)
+                to_pal(swapped, j).start()
+
+            for place, (from_pal, h) in enumerate(crossing_order(heads)):
+                if from_pal:
+                    at = place + (3 if h < heads - 3 else 2)
+                    pl.when(i == at)(lambda h=h: relay(h))
 
         nearby = i - heads
 
         @pl.when(jnp.logical_and(is_near, jnp.logical_and(nearby >= heads - NEAR, nearby < heads)))
         def _():
             send_q(nearby).wait_recv()
-            share(nearby)
+            share(nearby, guest_q[nearby], (2, 6), share_out.at[nearby], stat_out.at[nearby])
             for copy in send_share(nearby):
                 copy.start()
 
-        @pl.when(i == 2 * heads - jnp.where(jnp.logical_and(is_cut_row, group == 0), 1, 0))
+        @pl.when(jnp.logical_and(is_cut_row, jnp.logical_and(nearby >= tail, nearby < heads)))
+        def _():
+            index = nearby - tail
+            send_pal(q_s.at[nearby], pal_q.at[index], 0, index).wait_recv()
+            share(nearby, pal_q[index], (far,), pal_share_out.at[index], pal_stat_out.at[index])
+            for copy in send_pal_share(index):
+                copy.start()
+
+        @pl.when(i == 2 * heads - jnp.where(jnp.logical_and(is_cut_row, group == 1), 0, 1))
         def _():
             pltpu.make_async_copy(w_hbm, w_s, w_sem).wait()
             recv_att(0, early_heads, 0)
@@ -677,6 +726,20 @@
         def _():
             hold(i, *attend(q_s[i], (row_base, row_base + 1), i))
 
+        @pl.when(jnp.logical_and(i < heads, role == 0))
+        def _():
+            lend_q(i).wait_recv()
+            share(i, share_in[i], (1,), share_out.at[i], stat_out.at[i])
+            for copy in send_share(i, up_down_device):
+                copy.start()
+
+        @pl.when(jnp.logical_and(ready(i - last), is_near))
+        def _():
+            h = i - last
+            for copy in send_share(h):
+                copy.wait_recv()
+            hold(h, *merge(h, share_in.at[h], stat_in.at[h]))
+
         @pl.when(jnp.logical_and(role == 0, i == 2))
         def _():
             for h in range(heads - NEAR, heads):
@@ -690,44 +753,51 @@
             @pl.when(jnp.logical_and(i >= heads, i < 2 * heads))
             def _():
                 arrive(jnp.where(h == last, swapped, straight), h)
-                hold(h, *attend_more((4, 5), h))
+                pl.when(jnp.logical_and(role == 0, h == last))(lambda: up_down(swapped, h, way=3).start())
+                state = attend_more((4, 5), h)
+                pl.when(role == 0)(lambda: finish(h, *state))
+                pl.when(is_corner)(lambda: hold(h, *state))
 
             ending = i - heads - 2
-
-            @pl.when(jnp.logical_and(ready(ending), role == 0))
-            def _():
-                finish(ending, None, l_s[ending], acc_s[ending])
 
             @pl.when(jnp.logical_and(ready(ending), is_corner))
             def _():
                 for copy in send_share(ending):
                     copy.wait_recv()
-                merge(ending)
+                finish(ending, *merge(ending, share_in.at[ending], stat_in.at[ending]))
 
         ending = i - heads - 1
 
-        @pl.when(jnp.logical_and(ready(ending), is_cut_row))
-        def _():
-            split_or_whole(ending == last, lambda part: arrive(pal_far, ending, part, LAST_FAR))
-
         @pl.when(jnp.logical_and(ready(ending), is_near))
         def _():
-            arrive(1, ending)
             pl.when(ending == last)(lambda: arrive(5, ending))
-            finish(ending, *attend_more((1, 5, 6, 7), ending))
+            hold(ending, *attend_more((5, 6), ending))
 
         @pl.when(jnp.logical_and(ready(ending), is_host))
         def _():
-            @pl.when(ending < heads - NEAR)
+            @pl.when(ending < tail)
             def _():
                 send_q(ending).wait_recv()
-                share(ending)
+                arrive(6, ending)
+                share(ending, guest_q[ending], (2, 6), share_out.at[ending], stat_out.at[ending])
                 for copy in send_share(ending):
                     copy.start()
 
-            finish(ending, *attend_more((6, 7), ending))
-
-    pl.when(is_outer_row)(lambda: send_att(last).start())
+            hold(ending, *attend_more((7,), ending))
+
+        @pl.when(jnp.logical_and(is_cut_row, jnp.logical_and(ending >= 0, ending < tail)))
+        def _():
+            pl.when(is_near)(lambda: arrive(7, ending))
+            finish(ending, *attend_more((pal_far,), ending))
+
+        @pl.when(jnp.logical_and(is_cut_row, jnp.logical_and(ending >= tail, ending < heads)))
+        def _():
+            index = ending - tail
+            for copy in send_pal_share(index):
+                copy.wait_recv()
+            finish(ending, *merge(ending, pal_share_in.at[index], pal_stat_in.at[index]))
+
+    pl.when(is_corner)(lambda: send_att(last).start())
     recv_att(early_heads, heads, 1)
     for columns, value in mix(early_heads, heads):
         out_ref[:, columns] = (mixed_s[:, columns] + value).astype(out_ref.dtype)
@@ -753,15 +823,22 @@
             device_id_type=MESH,
         ).wait_send()
 
-    drain(0, 2)
+    pl.when(is_outer_row)(lambda: drain(0, 2))
+
+    @pl.when(is_cut_row)
+    def _():
+        drain_rows(kv.at[pl.ds(0, 2), pl.ds(0, heads - NEAR // 2)], send_sem.at[0])
+        drain_rows(pal_q, pal_send_sem.at[0])
+        drain_rows(pal_share_out, pal_send_sem.at[1])
+        drain_rows(pal_stat_out, pal_send_sem.at[2])
+
     drain(1, 1)
     drain_rows(other_s, att_send_sem)
-    pl.when(role == 0)(lambda: drain(1, 1))
+    pl.when(role == 0)(lambda: drain_rows(kv.at[0, 0], send_sem.at[3]))
     pl.when(role == 0)(lambda: drain_rows(guest_q.at[pl.ds(0, NEAR)], q_send_sem))
-    pl.when(is_corner)(lambda: drain_rows(q_s, q_send_sem))
+    pl.when(jnp.logical_or(is_corner, is_near))(lambda: drain_rows(q_s, q_send_sem))
     pl.when(is_cut_row)(lambda: drain(2, 2))
-    pl.when(is_host)(lambda: drain_rows(kv.at[0, 0], send_sem.at[3]))
-    for count, sender in ((heads - NEAR, is_host), (NEAR, is_near)):
+    for count, sender in ((heads, role == 0), (heads - NEAR, is_host), (NEAR, is_near)):
         pl.when(sender)(lambda count=count: drain_rows(share_out.at[pl.ds(0, count)], share_send_sem.at[0]))
         pl.when(sender)(lambda count=count: drain_rows(stat_out.at[pl.ds(0, count)], share_send_sem.at[1]))
 
@@ -792,6 +869,11 @@
             pltpu.VMEM((heads, rows, HD), jnp.bfloat16),
             pltpu.VMEM((heads, 8, rows), jnp.float32),
             pltpu.VMEM((heads, 8, rows), jnp.float32),
+            pltpu.VMEM((NEAR, rows, HD), jnp.bfloat16),
+            pltpu.VMEM((NEAR, rows, HD), jnp.bfloat16),
+            pltpu.VMEM((NEAR, rows, HD), jnp.bfloat16),
+            pltpu.VMEM((NEAR, 8, rows), jnp.float32),
+            pltpu.VMEM((NEAR, 8, rows), jnp.float32),
             dma((heads,)),
             dma,
             dma,
@@ -801,6 +883,8 @@
             dma((heads,)),
             dma((2,)),
             dma((2, heads)),
+            dma((3,)),
+            dma((3, NEAR)),
             dma,
             dma((2,)),
         ],
@@ -843,7 +927,8 @@
 
 
 def per_device(query_states, key_states, value_states, out_weight):
-    call = balanced_call if lax.axis_size("tm") == 4 * TCOLS else general_call
+    two_times = lax.axis_size("tm") == 4 * TCOLS and query_states.shape[2] >= 4 * HD
+    call = balanced_call if two_times else general_call
     return call(query_states, key_states, value_states, out_weight)
 
 

time: 67.1 us -> 65.2 us (0.972)
  the two profiles are of different devices: /device:TPU:0 before, /device:TPU:5 now
where the time goes in v4:
time: 65.2 us; the launch traced here: 65 us
  Pallas kernels  64 us (98%)
  local copies, waits for them, and re-layouts  1.02 us (2%)
    pallas_call x1, Pallas kernels, balanced_call(): pl.pallas_call(functools.partial(balanced_kernel, tiles), out_shape=jax.S...  64 us

profile of v4, /device:TPU:5, one launch (start us, length us, event | category | flops | bytes accessed | tf_op | source)
XLA Modules:
  0.0 65.0 jit_solution(12008711912672118734)
XLA Ops:
  0.0 64.0 %shard_map.46 = bf16[192,3072]{1,0:T(8,128)(2,1)S(1)} custom-call(bf16[1,384,768]{2,1,0:T(8,128)(2,1)} %q_hbm.1, bf16[1,384,768]{2,1,0:T(8,128)(2,1)} %k_hbm.1, bf16[1,384,768]{2,1,0:T(8,128)(2,1)} %v_hbm.1, bf16[1536,3072]{1,0:T(8,128)(2,1)} %w_hbm.1), custom_call_target="tpu_custom_call" | custom-call | tf_op jit(solution)/shard_map/pallas_call | solution.py:852
  64.0 1.0 %copy.6 = bf16[192,3072]{1,0:T(8,128)(2,1)} copy(bf16[192,3072]{1,0:T(8,128)(2,1)S(1)} %shard_map.46) | data formatting | bytes 2359296

commit v5 on v4

--- a/solution.py
+++ b/solution.py
@@ -373,6 +373,7 @@
     half = rows // 2
     last = heads - 1
     early_heads = heads - 3
+    first_heads = heads - 4
     tail = heads - NEAR
     me = lax.axis_index("tm")
     group = lax.rem(me, 2)
@@ -518,7 +519,7 @@
             src_ref=done_s.at[h, their_half],
             dst_ref=other_s.at[h],
             send_sem=att_send_sem,
-            recv_sem=att_recv_sem.at[jnp.where(h < early_heads, 0, 1)],
+            recv_sem=att_recv_sem.at[jnp.where(h < first_heads, 0, jnp.where(h < early_heads, 1, 2))],
             device_id={"tm": other_core},
             device_id_type=MESH,
         )
@@ -630,6 +631,10 @@
     def ready(h):
         return jnp.logical_and(h >= 0, h < heads)
 
+    is_slow = jnp.logical_and(is_cut_row, group == 0)
+    mix_at = 2 * heads - jnp.where(is_slow, 3, jnp.where(is_cut_row, 0, 1))
+    mix_gap = is_slow.astype(jnp.int32)
+
     @pl.loop(0, 2 * heads + 2)
     def _(i):
         settled = jnp.where(
@@ -637,6 +642,19 @@
         )
         settles = jnp.logical_and(ready(settled), jnp.logical_or(role != 0, i <= 2 * heads))
         pl.when(settles)(lambda: send_att(settled).start())
+
+        @pl.when(i == mix_at)
+        def _():
+            pltpu.make_async_copy(w_hbm, w_s, w_sem).wait()
+            recv_att(0, first_heads, 0)
+            for columns, value in mix(0, first_heads):
+                mixed_s[:, columns] = value
+
+        @pl.when(i == mix_at + mix_gap)
+        def _():
+            recv_att(first_heads, early_heads, 1)
+            for columns, value in mix(first_heads, early_heads):
+                mixed_s[:, columns] += value
 
         @pl.when(jnp.logical_and(i < heads, jnp.logical_or(is_outer_row, i > 0)))
         def _():
@@ -710,13 +728,6 @@
             for copy in send_pal_share(index):
                 copy.start()
 
-        @pl.when(i == 2 * heads - jnp.where(jnp.logical_and(is_cut_row, group == 1), 0, 1))
-        def _():
-            pltpu.make_async_copy(w_hbm, w_s, w_sem).wait()
-            recv_att(0, early_heads, 0)
-            for columns, value in mix(0, early_heads):
-                mixed_s[:, columns] = value
-
         @pl.when(jnp.logical_and(i >= 1, i <= heads))
         def _():
             for which in range(2):
@@ -768,29 +779,33 @@
 
         ending = i - heads - 1
 
-        @pl.when(jnp.logical_and(ready(ending), is_near))
+        is_whole = jnp.logical_and(ending >= 0, ending < tail)
+        is_tail = jnp.logical_and(ending >= tail, ending < heads)
+
+        @pl.when(jnp.logical_and(is_whole, is_near))
+        def _():
+            arrive(7, ending)
+            finish(ending, *attend_more((5, 6, 7), ending))
+
+        @pl.when(jnp.logical_and(is_whole, is_host))
+        def _():
+            send_q(ending).wait_recv()
+            arrive(6, ending)
+            share(ending, guest_q[ending], (2, 6), share_out.at[ending], stat_out.at[ending])
+            for copy in send_share(ending):
+                copy.start()
+            finish(ending, *attend_more((6, 7), ending))
+
+        @pl.when(jnp.logical_and(is_tail, is_near))
         def _():
             pl.when(ending == last)(lambda: arrive(5, ending))
             hold(ending, *attend_more((5, 6), ending))
 
-        @pl.when(jnp.logical_and(ready(ending), is_host))
-        def _():
-            @pl.when(ending < tail)
-            def _():
-                send_q(ending).wait_recv()
-                arrive(6, ending)
-                share(ending, guest_q[ending], (2, 6), share_out.at[ending], stat_out.at[ending])
-                for copy in send_share(ending):
-                    copy.start()
-
+        @pl.when(jnp.logical_and(is_tail, is_host))
+        def _():
             hold(ending, *attend_more((7,), ending))
 
-        @pl.when(jnp.logical_and(is_cut_row, jnp.logical_and(ending >= 0, ending < tail)))
-        def _():
-            pl.when(is_near)(lambda: arrive(7, ending))
-            finish(ending, *attend_more((pal_far,), ending))
-
-        @pl.when(jnp.logical_and(is_cut_row, jnp.logical_and(ending >= tail, ending < heads)))
+        @pl.when(jnp.logical_and(is_cut_row, is_tail))
         def _():
             index = ending - tail
             for copy in send_pal_share(index):
@@ -798,7 +813,7 @@
             finish(ending, *merge(ending, pal_share_in.at[index], pal_stat_in.at[index]))
 
     pl.when(is_corner)(lambda: send_att(last).start())
-    recv_att(early_heads, heads, 1)
+    recv_att(early_heads, heads, 2)
     for columns, value in mix(early_heads, heads):
         out_ref[:, columns] = (mixed_s[:, columns] + value).astype(out_ref.dtype)
 
@@ -886,7 +901,7 @@
             dma((3,)),
             dma((3, NEAR)),
             dma,
-            dma((2,)),
+            dma((3,)),
         ],
         compiler_params=pltpu.CompilerParams(
             collective_id=0, has_side_effects=True, vmem_limit_bytes=40 * 1024 * 1024
@@ -927,7 +942,7 @@
 
 
 def per_device(query_states, key_states, value_states, out_weight):
-    two_times = lax.axis_size("tm") == 4 * TCOLS and query_states.shape[2] >= 4 * HD
+    two_times = lax.axis_size("tm") == 4 * TCOLS and query_states.shape[2] >= 5 * HD
     call = balanced_call if two_times else general_call
     return call(query_states, key_states, value_states, out_weight)
 

time: 65.2 us -> 65 us (level)
  no operation moved by 1% of the time
where the time goes in v5:
time: 65 us; the launch traced here: 64.5 us
  Pallas kernels  63.5 us (98%)
  local copies, waits for them, and re-layouts  1.02 us (2%)
    pallas_call x1, Pallas kernels, balanced_call(): pl.pallas_call(functools.partial(balanced_kernel, tiles), out_shape=jax.S...  63.5 us

profile of v5, /device:TPU:5, one launch (start us, length us, event | category | flops | bytes accessed | tf_op | source)
XLA Modules:
  0.0 64.5 jit_solution(9431674447327071604)
XLA Ops:
  0.0 63.5 %shard_map.46 = bf16[192,3072]{1,0:T(8,128)(2,1)S(1)} custom-call(bf16[1,384,768]{2,1,0:T(8,128)(2,1)} %q_hbm.1, bf16[1,384,768]{2,1,0:T(8,128)(2,1)} %k_hbm.1, bf16[1,384,768]{2,1,0:T(8,128)(2,1)} %v_hbm.1, bf16[1536,3072]{1,0:T(8,128)(2,1)} %w_hbm.1), custom_call_target="tpu_custom_call" | custom-call | tf_op jit(solution)/shard_map/pallas_call | solution.py:867
  63.5 1.0 %copy.6 = bf16[192,3072]{1,0:T(8,128)(2,1)} copy(bf16[192,3072]{1,0:T(8,128)(2,1)S(1)} %shard_map.46) | data formatting | bytes 2359296

commit v6 on v5

--- a/solution.py
+++ b/solution.py
@@ -413,12 +413,8 @@
     def load_w(h, which):
         owner = group if which == 0 else 1 - group
         source = pl.ds(pl.multiple_of((owner * heads + h) * HD, HD), HD)
-        target = pl.ds(pl.multiple_of((2 * h + which) * HD, HD), HD)
+        target = pl.ds(pl.multiple_of((which * heads + h) * HD, HD), HD)
         return pltpu.make_async_copy(w_hbm.at[source], w_s.at[target], w_sem)
-
-    for h in (last, *range(last)):
-        for copy in load(jnp.int32(h)):
-            copy.start()
 
     barrier = pltpu.get_barrier_semaphore()
 
@@ -430,6 +426,9 @@
     greet(up_down_device)
     pl.when(is_cut_row)(lambda: greet(cut_device))
     pl.when(is_corner)(lambda: greet(device_of(2)))
+    for h in (last, *range(last)):
+        for copy in load(jnp.int32(h)):
+            copy.start()
     pl.semaphore_wait(barrier, 3 + is_cut_row.astype(jnp.int32) + is_near.astype(jnp.int32))
 
     def transfer(way, slot, h, target, device, part=None, kind=0, landing=0):
@@ -445,8 +444,8 @@
     def arrive(slot, h, part=None, kind=0):
         transfer(0, slot, h, slot, pal_device, part, kind, role).wait_recv()
 
-    def to_pal(slot, h, part=None, kind=0):
-        return transfer(0, slot, h, slot, pal_device, part, kind, pal)
+    def to_pal(slot, h, part=None, kind=0, way=0):
+        return transfer(way, slot, h, slot, pal_device, part, kind, pal)
 
     def up_down(slot, h, way=1):
         return transfer(way, slot, h, slot, up_down_device)
@@ -546,13 +545,12 @@
 
             @pl.when(is_corner)
             def _():
-                for near in range(heads - NEAR, heads):
-                    send_q(near, device=pal_device).start()
+                send_q(last, device=pal_device).start()
     send_own(last)
 
     @pl.when(is_corner)
     def _():
-        for h in range(heads - NEAR):
+        for h in (*range(tail, last), *range(tail)):
             send_q(h).start()
 
     @pl.when(is_near)
@@ -616,17 +614,21 @@
     width = out_ref.shape[1]
     chunk = OUT_CHUNK
 
-    def mix(first, stop):
+    def half_mix(which, first, stop):
         lhs = jnp.concatenate(
-            [part for h in range(first, stop) for part in (done_s[h, own_half, :], other_s[h])], axis=1
-        )
-        depth = slice(2 * first * HD, 2 * stop * HD)
+            [other_s[h] if which else done_s[h, own_half, :] for h in range(first, stop)], axis=1
+        )
+        depth = slice((which * heads + first) * HD, (which * heads + stop) * HD)
 
         def product(n):
             columns = pl.ds(n * chunk, chunk)
             return columns, jnp.dot(lhs, w_s[depth, columns], preferred_element_type=jnp.float32)
 
         return (product(n) for n in range(width // chunk))
+
+    def mix(first, stop):
+        for (columns, own), (_, other) in zip(half_mix(0, first, stop), half_mix(1, first, stop)):
+            yield columns, own + other
 
     def ready(h):
         return jnp.logical_and(h >= 0, h < heads)
@@ -641,7 +643,9 @@
             jnp.logical_and(role == 0, i == heads + 1), last, i - heads - jnp.where(is_corner, 3, 2)
         )
         settles = jnp.logical_and(ready(settled), jnp.logical_or(role != 0, i <= 2 * heads))
-        pl.when(settles)(lambda: send_att(settled).start())
+        held = jnp.logical_and(is_near, settled == tail - 1)
+        pl.when(jnp.logical_and(settles, jnp.logical_not(held)))(lambda: send_att(settled).start())
+        pl.when(jnp.logical_and(is_near, i == 2 * heads))(lambda: send_att(tail - 1).start())
 
         @pl.when(i == mix_at)
         def _():
@@ -685,7 +689,7 @@
                 else:
                     arrive(far, h)
                     if h < tail:
-                        to_pal(far, h).start()
+                        to_pal(far, h, way=3).start()
 
             at = 0
             for place, (from_pal, h) in enumerate(crossing_order(heads)):
@@ -753,12 +757,25 @@
 
         @pl.when(jnp.logical_and(role == 0, i == 2))
         def _():
-            for h in range(heads - NEAR, heads):
+            send_q(last).wait_recv()
+            send_q(last, source=guest_q).start()
+
+        @pl.when(jnp.logical_and(is_host, i == heads))
+        def _():
+            for h in range(tail, last):
                 send_q(h).wait_recv()
-                send_q(h, source=guest_q).start()
+                send_q(h, source=guest_q, device=pal_device).start()
 
         @pl.when(is_outer_row)
         def _():
+            ending = i - heads - 2
+
+            @pl.when(jnp.logical_and(ready(ending), is_corner))
+            def _():
+                for copy in send_share(ending):
+                    copy.wait_recv()
+                finish(ending, *merge(ending, share_in.at[ending], stat_in.at[ending]))
+
             h = jnp.where(i == heads, last, i - heads - 1)
 
             @pl.when(jnp.logical_and(i >= heads, i < 2 * heads))
@@ -769,23 +786,17 @@
                 pl.when(role == 0)(lambda: finish(h, *state))
                 pl.when(is_corner)(lambda: hold(h, *state))
 
-            ending = i - heads - 2
-
-            @pl.when(jnp.logical_and(ready(ending), is_corner))
-            def _():
-                for copy in send_share(ending):
-                    copy.wait_recv()
-                finish(ending, *merge(ending, share_in.at[ending], stat_in.at[ending]))
-
         ending = i - heads - 1
 
         is_whole = jnp.logical_and(ending >= 0, ending < tail)
         is_tail = jnp.logical_and(ending >= tail, ending < heads)
 
-        @pl.when(jnp.logical_and(is_whole, is_near))
-        def _():
-            arrive(7, ending)
-            finish(ending, *attend_more((5, 6, 7), ending))
+        waiting = jnp.where(i == 2 * heads - 1, tail - 1, ending)
+
+        @pl.when(jnp.logical_and(jnp.logical_and(waiting >= 0, waiting < tail), jnp.logical_and(is_near, i != heads + tail)))
+        def _():
+            arrive(7, waiting)
+            finish(waiting, *attend_more((5, 6, 7), waiting))
 
         @pl.when(jnp.logical_and(is_whole, is_host))
         def _():
@@ -813,8 +824,10 @@
             finish(ending, *merge(ending, pal_share_in.at[index], pal_stat_in.at[index]))
 
     pl.when(is_corner)(lambda: send_att(last).start())
+    for columns, value in half_mix(0, early_heads, heads):
+        mixed_s[:, columns] += value
     recv_att(early_heads, heads, 2)
-    for columns, value in mix(early_heads, heads):
+    for columns, value in half_mix(1, early_heads, heads):
         out_ref[:, columns] = (mixed_s[:, columns] + value).astype(out_ref.dtype)
 
     def drain(way, count):
@@ -842,7 +855,8 @@
 
     @pl.when(is_cut_row)
     def _():
-        drain_rows(kv.at[pl.ds(0, 2), pl.ds(0, heads - NEAR // 2)], send_sem.at[0])
+        drain(0, 1)
+        drain_rows(kv.at[0, pl.ds(0, tail)], send_sem.at[3])
         drain_rows(pal_q, pal_send_sem.at[0])
         drain_rows(pal_share_out, pal_send_sem.at[1])
         drain_rows(pal_stat_out, pal_send_sem.at[2])
@@ -850,7 +864,8 @@
     drain(1, 1)
     drain_rows(other_s, att_send_sem)
     pl.when(role == 0)(lambda: drain_rows(kv.at[0, 0], send_sem.at[3]))
-    pl.when(role == 0)(lambda: drain_rows(guest_q.at[pl.ds(0, NEAR)], q_send_sem))
+    pl.when(role == 0)(lambda: drain_rows(guest_q.at[0], q_send_sem))
+    pl.when(is_host)(lambda: drain_rows(guest_q.at[pl.ds(0, NEAR - 1)], q_send_sem))
     pl.when(jnp.logical_or(is_corner, is_near))(lambda: drain_rows(q_s, q_send_sem))
     pl.when(is_cut_row)(lambda: drain(2, 2))
     for count, sender in ((heads, role == 0), (heads - NEAR, is_host), (NEAR, is_near)):

time: 65 us -> 64.5 us (level)
  Pallas kernels: 63.5 us -> 62.8 us
    pallas_call x1, Pallas kernels: 63.5 us -> 62.8 us  [balanced_call(): pl.pallas_call(functools.partial(balanced_kernel, tiles), out_shape=jax.S...]
where the time goes in v6:
time: 64.5 us; the launch traced here: 63.8 us
  Pallas kernels  62.8 us (97%)
  local copies, waits for them, and re-layouts  1.02 us (2%)
    pallas_call x1, Pallas kernels, balanced_call(): pl.pallas_call(functools.partial(balanced_kernel, tiles), out_shape=jax.S...  62.8 us

profile of v6, /device:TPU:5, one launch (start us, length us, event | category | flops | bytes accessed | tf_op | source)
XLA Modules:
  0.0 63.8 jit_solution(4911164514493350336)
XLA Ops:
  0.0 62.8 %shard_map.46 = bf16[192,3072]{1,0:T(8,128)(2,1)S(1)} custom-call(bf16[1,384,768]{2,1,0:T(8,128)(2,1)} %q_hbm.1, bf16[1,384,768]{2,1,0:T(8,128)(2,1)} %k_hbm.1, bf16[1,384,768]{2,1,0:T(8,128)(2,1)} %v_hbm.1, bf16[1536,3072]{1,0:T(8,128)(2,1)} %w_hbm.1), custom_call_target="tpu_custom_call" | custom-call | tf_op jit(solution)/shard_map/pallas_call | solution.py:882
  62.8 1.0 %copy.6 = bf16[192,3072]{1,0:T(8,128)(2,1)} copy(bf16[192,3072]{1,0:T(8,128)(2,1)S(1)} %shard_map.46) | data formatting | bytes 2359296

commit v7 on v6

--- a/solution.py
+++ b/solution.py
@@ -634,8 +634,8 @@
         return jnp.logical_and(h >= 0, h < heads)
 
     is_slow = jnp.logical_and(is_cut_row, group == 0)
-    mix_at = 2 * heads - jnp.where(is_slow, 3, jnp.where(is_cut_row, 0, 1))
-    mix_gap = is_slow.astype(jnp.int32)
+    mix_at = 2 * heads - jnp.where(is_slow, 3, 1)
+    mix_gap = is_cut_row.astype(jnp.int32)
 
     @pl.loop(0, 2 * heads + 2)
     def _(i):

time: 64.5 us -> 64.5 us (level)
  no operation moved by 1% of the time
where the time goes in v7:
time: 64.5 us; the launch traced here: 63.8 us
  Pallas kernels  62.7 us (97%)
  local copies, waits for them, and re-layouts  1.02 us (2%)
    pallas_call x1, Pallas kernels, balanced_call(): pl.pallas_call(functools.partial(balanced_kernel, tiles), out_shape=jax.S...  62.7 us

profile of v7, /device:TPU:5, one launch (start us, length us, event | category | flops | bytes accessed | tf_op | source)
XLA Modules:
  0.0 63.8 jit_solution(5883015988232710141)
XLA Ops:
  0.0 62.7 %shard_map.46 = bf16[192,3072]{1,0:T(8,128)(2,1)S(1)} custom-call(bf16[1,384,768]{2,1,0:T(8,128)(2,1)} %q_hbm.1, bf16[1,384,768]{2,1,0:T(8,128)(2,1)} %k_hbm.1, bf16[1,384,768]{2,1,0:T(8,128)(2,1)} %v_hbm.1, bf16[1536,3072]{1,0:T(8,128)(2,1)} %w_hbm.1), custom_call_target="tpu_custom_call" | custom-call | tf_op jit(solution)/shard_map/pallas_call | solution.py:882
  62.8 1.0 %copy.6 = bf16[192,3072]{1,0:T(8,128)(2,1)} copy(bf16[192,3072]{1,0:T(8,128)(2,1)S(1)} %shard_map.46) | data formatting | bytes 2359296

commit v8 on v7

--- a/solution.py
+++ b/solution.py
@@ -431,27 +431,31 @@
             copy.start()
     pl.semaphore_wait(barrier, 3 + is_cut_row.astype(jnp.int32) + is_near.astype(jnp.int32))
 
+    def row_of(slot):
+        return jnp.where(slot < 4, lax.div(slot, 2), slot - 2)
+
     def transfer(way, slot, h, target, device, part=None, kind=0, landing=0):
+        slot, target = jnp.int32(slot), jnp.int32(target)
         return pltpu.make_async_remote_copy(
             src_ref=kv.at[slot, h] if part is None else kv.at[slot, h, part],
             dst_ref=kv.at[target, h] if part is None else kv.at[target, h, part],
             send_sem=send_sem.at[way],
-            recv_sem=recv_sem.at[landing, kind] if part == 1 else recv_sem.at[target, h],
+            recv_sem=recv_sem.at[landing, kind] if part == 1 else recv_sem.at[row_of(target), h],
             device_id={"tm": device},
             device_id_type=MESH,
         )
 
     def arrive(slot, h, part=None, kind=0):
-        transfer(0, slot, h, slot, pal_device, part, kind, role).wait_recv()
+        transfer(0, slot, h, slot, pal_device, part, kind, 2 + side).wait_recv()
 
     def to_pal(slot, h, part=None, kind=0, way=0):
-        return transfer(way, slot, h, slot, pal_device, part, kind, pal)
+        return transfer(way, slot, h, slot, pal_device, part, kind, 3 - side)
 
     def up_down(slot, h, way=1):
         return transfer(way, slot, h, slot, up_down_device)
 
     def cross(slot, h, part=None, kind=0):
-        return transfer(2, slot, h, tiles - 1 - slot, cut_device, part, kind, pal)
+        return transfer(2, slot, h, tiles - 1 - slot, cut_device, part, kind, 3 - side)
 
     def split_or_whole(is_split, act):
         pl.when(jnp.logical_not(is_split))(lambda: act(None))
@@ -908,7 +912,7 @@
             dma,
             dma,
             dma((4,)),
-            dma((tiles, heads)),
+            dma((tiles - 2, heads)),
             dma,
             dma((heads,)),
             dma((2,)),

time: 64.5 us -> 64.5 us (level)
  no operation moved by 1% of the time
where the time goes in v8:
time: 64.5 us; the launch traced here: 63.7 us
  Pallas kernels  62.7 us (97%)
  local copies, waits for them, and re-layouts  1.02 us (2%)
    pallas_call x1, Pallas kernels, balanced_call(): pl.pallas_call(functools.partial(balanced_kernel, tiles), out_shape=jax.S...  62.7 us

profile of v8, /device:TPU:5, one launch (start us, length us, event | category | flops | bytes accessed | tf_op | source)
XLA Modules:
  0.0 63.7 jit_solution(9666795564643618703)
XLA Ops:
  0.0 62.7 %shard_map.46 = bf16[192,3072]{1,0:T(8,128)(2,1)S(1)} custom-call(bf16[1,384,768]{2,1,0:T(8,128)(2,1)} %q_hbm.1, bf16[1,384,768]{2,1,0:T(8,128)(2,1)} %k_hbm.1, bf16[1,384,768]{2,1,0:T(8,128)(2,1)} %v_hbm.1, bf16[1536,3072]{1,0:T(8,128)(2,1)} %w_hbm.1), custom_call_target="tpu_custom_call" | custom-call | tf_op jit(solution)/shard_map/pallas_call | solution.py:886
  62.7 1.0 %copy.6 = bf16[192,3072]{1,0:T(8,128)(2,1)} copy(bf16[192,3072]{1,0:T(8,128)(2,1)S(1)} %shard_map.46) | data formatting | bytes 2359296
